TPU v7x, 32 devices: a whole 2x2x4 slice. The times are simulated.
32 devices in a mesh: grp: 2 (over x), tm: 16 (over z, y, core).
Axes of the slice: x: 2, y: 2, z: 4, core: 2. Of those that a mesh axis runs over, the one named last changes fastest.
Arguments:
- dyn_a: float32 [128, 4, 64, 64], P('tm', 'grp'), parts along dimension 1, may hold values from -1 to 1
- dyn_b: float32 [128, 4, 64, 32], P('tm', 'grp'), parts along dimension 1, may hold values from -0.109375 to 0.109375
- gains: float32 [128, 4, 32, 64], P('tm', 'grp'), parts along dimension 1, may hold values from -0.2 to 0.2
- defects: float32 [128, 4, 64], P('tm', 'grp'), parts along dimension 1, may hold values from -6 to 6
- state_grad: float32 [128, 4, 64], P('tm', 'grp'), parts along dimension 1, may hold values from -6 to 6
- control_grad: float32 [128, 4, 32], P('tm', 'grp'), parts along dimension 1, may hold values from -1.5 to 1.5
- cost_factor: float32 [64, 64], replicated, may hold values from -0.75 to 0.75
- control_factor: float32 [32, 32], replicated, may hold values from -1 to 1
- init_state: float32 [4, 64], P('grp'), parts along dimension 0, may hold values from -6 to 6
Outputs:
- new_gains: float32 [128, 4, 32, 64], P('tm', 'grp'), parts along dimension 1
- feedforward: float32 [128, 4, 32], P('tm', 'grp'), parts along dimension 1
- states: float32 [128, 4, 64], P('tm', 'grp'), parts along dimension 1
- controls: float32 [128, 4, 32], P('tm', 'grp'), parts along dimension 1
- decrease: float32 [4], P('grp'), parts along dimension 0
There are 2 independent parts, one for each index of `grp`. A program takes and returns all parts, laid end to end along the dimension named above; an argument that names none is the same for every part. Nothing has to cross between parts.
All inputs are finite; a program needn't handle non-finite values.
Results may differ from a plain program's by a relative error of at most 0.0003.
Values sent between devices are 32-bit elements; how exact they have to be, the bound alone decides.
A program may use at most 64 MiB of HBM per device.

v0:
```python
import math

import jax
import jax.numpy as jnp
from jax import lax
from jax.sharding import PartitionSpec as P


def carried_in(part, axis, combine, identity, reverse):
    count = lax.axis_size(axis)
    place = lax.axis_index(axis)
    ahead = count - 1 - place if reverse else place
    gathered = jax.tree.map(lambda a: lax.all_gather(a, axis), part)
    state = jax.tree.map(lambda a, e: jnp.zeros_like(a) + jnp.asarray(e, a.dtype), part, identity)

    def one(turn, state):
        source = count - 1 - turn if reverse else turn
        return combine(
            state, jax.tree.map(lambda a: lax.dynamic_index_in_dim(a, source, 0, False), gathered)
        )

    return lax.fori_loop(0, ahead, one, state)


def product(left, right):
    return jnp.matmul(left, right, precision=lax.Precision.HIGHEST)


def flipped(matrix):
    return jnp.swapaxes(matrix, -1, -2)


def apply_vec(matrix, vector):
    return product(matrix, vector[..., None])[..., 0]


def spd_solve(matrix, right_side):
    factor = jnp.linalg.cholesky(matrix)
    inner = jax.scipy.linalg.solve_triangular(factor, right_side, lower=True)
    return jax.scipy.linalg.solve_triangular(factor, inner, lower=True, trans=1)


def compose_value(later, earlier):
    f_late, q_late, h_late, g_late = later
    f_early, q_early, h_early, g_early = earlier
    merged_f = product(f_early, f_late)
    merged_q = product(flipped(f_late), product(q_early, f_late)) + q_late
    merged_h = h_early + apply_vec(f_early, h_late)
    merged_g = apply_vec(flipped(f_late), g_early + apply_vec(q_early, h_late)) + g_late
    return (merged_f, merged_q, merged_h, merged_g)


def value_combine(earlier, later):
    return compose_value(later, earlier)


def compose_state(earlier, later):
    m_early, c_early = earlier
    m_late, c_late = later
    return (product(m_late, m_early), apply_vec(m_late, c_early) + c_late)


def value_joined(lower, higher):
    return compose_value(lower, higher)


def state_joined(lower, higher):
    return compose_state(lower, higher)


def fold_tree(elems, joined):
    while elems[0].shape[0] > 1:
        count = elems[0].shape[0]
        half = count // 2
        lower = tuple((item[0 : 2 * half : 2] for item in elems))
        higher = tuple((item[1 : 2 * half : 2] for item in elems))
        merged = joined(lower, higher)
        elems = merged
    return tuple((item[0] for item in elems))


def fold_local(elems, joined):
    return fold_tree(elems, joined)


def shards(
    dyn_a, dyn_b, gains, defects, state_grad, control_grad, cost_factor, control_factor, init_state
):
    local_knots, trajs, width, controls_n = dyn_b.shape
    knots = local_knots * lax.axis_size("tm")
    scale = 1.0 / math.sqrt(knots)
    term_q = jnp.eye(width, dtype=jnp.float32) + product(cost_factor, flipped(cost_factor))
    run_q = term_q / knots
    run_r = jnp.eye(controls_n, dtype=jnp.float32) + product(
        control_factor, flipped(control_factor)
    )
    drift = defects * scale
    closed = dyn_a + product(dyn_b, gains)
    section_q = run_q + product(flipped(gains), product(run_r, gains))
    section_g = state_grad * scale + apply_vec(flipped(gains), control_grad)
    summary = fold_local((closed, section_q, drift, section_g), value_joined)
    count = trajs - 0
    identity = (
        jnp.broadcast_to(jnp.eye(width, dtype=jnp.float32), (count, width, width)),
        jnp.zeros((count, width, width), jnp.float32),
        jnp.zeros((count, width), jnp.float32),
        jnp.zeros((count, width), jnp.float32),
    )
    pre_f, pre_q, pre_h, pre_g = carried_in(summary, "tm", value_combine, identity, True)
    end_mat = product(flipped(pre_f), product(term_q, pre_f)) + pre_q
    end_vec = apply_vec(flipped(pre_f), apply_vec(term_q, pre_h)) + pre_g

    def back_step(carry, item):
        value_mat, value_vec = carry
        a_mat, b_mat, f_mat, q_mat, d_vec, g_vec, r_vec = item
        value_b = product(value_mat, b_mat)
        hess = run_r + product(flipped(b_mat), value_b)
        cross = product(flipped(value_b), a_mat)
        lin = r_vec + apply_vec(flipped(b_mat), apply_vec(value_mat, d_vec) + value_vec)
        solved = spd_solve(hess, jnp.concatenate([cross, lin[..., None]], -1))
        new_gain = -solved[..., :width]
        feed = -solved[..., width]
        change = jnp.sum(feed * lin, -1) + 0.5 * jnp.sum(feed * apply_vec(hess, feed), -1)
        step_m = a_mat + product(b_mat, new_gain)
        step_c = apply_vec(b_mat, feed) + d_vec
        next_mat = product(flipped(f_mat), product(value_mat, f_mat)) + q_mat
        next_vec = apply_vec(flipped(f_mat), value_vec + apply_vec(value_mat, d_vec)) + g_vec
        return ((next_mat, next_vec), (new_gain, feed, change, step_m, step_c))

    items = (dyn_a, dyn_b, closed, section_q, drift, section_g, control_grad)
    _, results = lax.scan(back_step, (end_mat, end_vec), items, reverse=True)
    new_gains, feedforward, changes, step_m, step_c = results
    decrease = lax.psum(jnp.sum(changes, 0), "tm") / knots
    state_summary = fold_local((step_m, step_c), state_joined)
    state_identity = (
        jnp.broadcast_to(jnp.eye(width, dtype=jnp.float32), (trajs, width, width)),
        jnp.zeros((trajs, width), jnp.float32),
    )
    prefix_m, prefix_c = carried_in(state_summary, "tm", compose_state, state_identity, False)
    start_state = apply_vec(prefix_m, init_state) + prefix_c

    def forward_step(state, item):
        a_mat, b_mat, new_gain, feed, d_vec = item
        control = apply_vec(new_gain, state) + feed
        following = apply_vec(a_mat, state) + apply_vec(b_mat, control) + d_vec
        return (following, (state, control))

    _, (states, controls) = lax.scan(
        forward_step, start_state, (dyn_a, dyn_b, new_gains, feedforward, drift)
    )
    return (new_gains, feedforward, states, controls, decrease)


def solution(mesh):
    in_specs = (
        P("tm", "grp", None, None),
        P("tm", "grp", None, None),
        P("tm", "grp", None, None),
        P("tm", "grp", None),
        P("tm", "grp", None),
        P("tm", "grp", None),
        P(),
        P(),
        P("grp", None),
    )
    out_specs = (
        P("tm", "grp", None, None),
        P("tm", "grp", None),
        P("tm", "grp", None),
        P("tm", "grp", None),
        P("grp"),
    )
    return jax.shard_map(shards, mesh=mesh, in_specs=in_specs, out_specs=out_specs, check_vma=False)
```

profile of v0, /device:TPU:0, one launch (start us, length us, event | category | flops | bytes accessed | tf_op | source)
XLA Modules:
  0.0 338.6 jit_solution(10951159836824277851)
XLA Ops:
  0.6 0.9 convolution_add_fusion.8
  2.7 1.1 fusion.91
  3.8 1.1 convolution_add_fusion.3
  4.9 0.6 fusion.100
  5.4 0.6 convolution_add_fusion.4
  11.0 23.1 %all_gather.21 = f32[16,2,64]{2,1,0:T(2,128)S(1)} all-gather(f32[1,2,64]{2,1,0:T(2,128)S(1)} %slice_add_fusion.9), channel_id=1, replica_groups=mesh['grp'=2,'tm'=16] {'tm'}, dimensions={0}, use_global_device_ids=true | all-gather | bytes 8704 | tf_op jit(solution)/shard_map/all_gather | solution.py:13
  34.8 21.9 %all_gather.19 = f32[16,2,64,64]{3,2,1,0:T(8,128)} all-gather(f32[1,2,64,64]{3,2,1,0:T(8,128)S(1)} %copy.85), channel_id=1, replica_groups=mesh['grp'=2,'tm'=16] {'tm'}, dimensions={0}, use_global_device_ids=true | all-gather | bytes 557056 | tf_op jit(solution)/shard_map/all_gather | solution.py:13
  56.9 19.3 %all_gather.20 = f32[16,2,64]{2,1,0:T(2,128)S(1)} all-gather(f32[1,2,64]{2,1,0:T(2,128)S(1)} %slice_add_fusion.11), channel_id=1, replica_groups=mesh['grp'=2,'tm'=16] {'tm'}, dimensions={0}, use_global_device_ids=true | all-gather | bytes 8704 | tf_op jit(solution)/shard_map/all_gather | solution.py:13
  76.4 20.7 %all-gather = f32[32,64,64]{2,1,0:T(8,128)S(1)} all-gather(f32[2,64,64]{2,1,0:T(8,128)S(1)} %fusion.135), channel_id=2, replica_groups=mesh['grp'=2,'tm'=16] {'tm'}, dimensions={0}, use_global_device_ids=true | all-gather | bytes 557056 | tf_op jit(solution)/shard_map/all_gather | solution.py:13
  97.2 36.0 %while.70 = (s32[]{:T(128)}, f32[2,64,64]{1,2,0:T(8,128)S(1)}, f32[2,64,64]{2,1,0:T(8,128)S(1)}, f32[2,64]{1,0:T(2,128)S(1)}, f32[2,64]{1,0:T(2,128)S(1)}, /*ind...) while((s32[]{:T(128)}, f32[2,64,64]{1,2,0:T(8,128)S(1)}, ...), condition=%wide.region_1.2_spmd, body=%wide.region_0.1_spmd.sunk | while | flops 19177860 | bytes 731335 | solution.py:22
  97.9 1.1 convolution_add_fusion.11
  100.3 1.1 convolution_add_fusion.11
  102.7 1.1 convolution_add_fusion.11
  105.1 1.1 convolution_add_fusion.11
  107.5 1.1 convolution_add_fusion.11
  109.9 1.1 convolution_add_fusion.11
  112.3 1.1 convolution_add_fusion.11
  114.7 1.1 convolution_add_fusion.11
  117.0 1.1 convolution_add_fusion.11
  119.4 1.1 convolution_add_fusion.11
  121.8 1.1 convolution_add_fusion.11
  124.2 1.1 convolution_add_fusion.11
  126.6 1.1 convolution_add_fusion.11
  129.0 1.1 convolution_add_fusion.11
  131.4 1.1 convolution_add_fusion.11
  134.3 117.8 %while.71 = (s32[]{:T(128)}, f32[2,64,64]{2,1,0:T(8,128)S(1)}, f32[2,64]{1,0:T(2,128)S(1)}, f32[8,2,32,64]{3,2,1,0:T(8,128)S(1)}, f32[8,2,32]{2,1,0:T(2,128)S(1)...) while((s32[]{:T(128)}, f32[2,64,64]{2,1,0:T(8,128)S(1)}, ...), condition=%wide.region_7.8_spmd, body=%wide.region_2.7_spmd.sunk | while | flops 27159488 | bytes 1454393 | solution.py:131
  134.9 5.9 %custom-call.25 = f32[2,32,32]{2,1,0:T(8,128)S(1)} custom-call(f32[2,32,32]{2,1,0:T(8,128)S(1)} %fusion.337), custom_call_target="Cholesky" | custom-call | tf_op jit(solution)/shard_map/while/body/eval_jaxpr/jit(cholesky)/cholesky | solution.py:38
  141.0 4.9 %custom-call.26 = f32[2,1,32,32]{2,3,1,0:T(8,128)S(1)} custom-call(f32[2,1,32,32]{3,2,1,0:T(8,128)S(1)} %select_bitcast_fusion.2), custom_call_target="InvertDiagBlocksLowerTriangular" | custom-call | tf_op jit(solution)/shard_map/while/body/eval_jaxpr/jit(_solve_triangular)/vmap()/triangular_solve | solution.py:40
  149.6 5.9 %custom-call.25 = f32[2,32,32]{2,1,0:T(8,128)S(1)} custom-call(f32[2,32,32]{2,1,0:T(8,128)S(1)} %fusion.337), custom_call_target="Cholesky" | custom-call | tf_op jit(solution)/shard_map/while/body/eval_jaxpr/jit(cholesky)/cholesky | solution.py:38
  155.8 4.9 %custom-call.26 = f32[2,1,32,32]{2,3,1,0:T(8,128)S(1)} custom-call(f32[2,1,32,32]{3,2,1,0:T(8,128)S(1)} %select_bitcast_fusion.2), custom_call_target="InvertDiagBlocksLowerTriangular" | custom-call | tf_op jit(solution)/shard_map/while/body/eval_jaxpr/jit(_solve_triangular)/vmap()/triangular_solve | solution.py:40
  164.4 5.9 %custom-call.25 = f32[2,32,32]{2,1,0:T(8,128)S(1)} custom-call(f32[2,32,32]{2,1,0:T(8,128)S(1)} %fusion.337), custom_call_target="Cholesky" | custom-call | tf_op jit(solution)/shard_map/while/body/eval_jaxpr/jit(cholesky)/cholesky | solution.py:38
  170.5 4.9 %custom-call.26 = f32[2,1,32,32]{2,3,1,0:T(8,128)S(1)} custom-call(f32[2,1,32,32]{3,2,1,0:T(8,128)S(1)} %select_bitcast_fusion.2), custom_call_target="InvertDiagBlocksLowerTriangular" | custom-call | tf_op jit(solution)/shard_map/while/body/eval_jaxpr/jit(_solve_triangular)/vmap()/triangular_solve | solution.py:40
  179.1 5.9 %custom-call.25 = f32[2,32,32]{2,1,0:T(8,128)S(1)} custom-call(f32[2,32,32]{2,1,0:T(8,128)S(1)} %fusion.337), custom_call_target="Cholesky" | custom-call | tf_op jit(solution)/shard_map/while/body/eval_jaxpr/jit(cholesky)/cholesky | solution.py:38
  185.2 4.9 %custom-call.26 = f32[2,1,32,32]{2,3,1,0:T(8,128)S(1)} custom-call(f32[2,1,32,32]{3,2,1,0:T(8,128)S(1)} %select_bitcast_fusion.2), custom_call_target="InvertDiagBlocksLowerTriangular" | custom-call | tf_op jit(solution)/shard_map/while/body/eval_jaxpr/jit(_solve_triangular)/vmap()/triangular_solve | solution.py:40
  193.8 5.9 %custom-call.25 = f32[2,32,32]{2,1,0:T(8,128)S(1)} custom-call(f32[2,32,32]{2,1,0:T(8,128)S(1)} %fusion.337), custom_call_target="Cholesky" | custom-call | tf_op jit(solution)/shard_map/while/body/eval_jaxpr/jit(cholesky)/cholesky | solution.py:38
  199.9 4.9 %custom-call.26 = f32[2,1,32,32]{2,3,1,0:T(8,128)S(1)} custom-call(f32[2,1,32,32]{3,2,1,0:T(8,128)S(1)} %select_bitcast_fusion.2), custom_call_target="InvertDiagBlocksLowerTriangular" | custom-call | tf_op jit(solution)/shard_map/while/body/eval_jaxpr/jit(_solve_triangular)/vmap()/triangular_solve | solution.py:40
  208.5 5.9 %custom-call.25 = f32[2,32,32]{2,1,0:T(8,128)S(1)} custom-call(f32[2,32,32]{2,1,0:T(8,128)S(1)} %fusion.337), custom_call_target="Cholesky" | custom-call | tf_op jit(solution)/shard_map/while/body/eval_jaxpr/jit(cholesky)/cholesky | solution.py:38
  214.6 4.9 %custom-call.26 = f32[2,1,32,32]{2,3,1,0:T(8,128)S(1)} custom-call(f32[2,1,32,32]{3,2,1,0:T(8,128)S(1)} %select_bitcast_fusion.2), custom_call_target="InvertDiagBlocksLowerTriangular" | custom-call | tf_op jit(solution)/shard_map/while/body/eval_jaxpr/jit(_solve_triangular)/vmap()/triangular_solve | solution.py:40
  223.2 5.9 %custom-call.25 = f32[2,32,32]{2,1,0:T(8,128)S(1)} custom-call(f32[2,32,32]{2,1,0:T(8,128)S(1)} %fusion.337), custom_call_target="Cholesky" | custom-call | tf_op jit(solution)/shard_map/while/body/eval_jaxpr/jit(cholesky)/cholesky | solution.py:38
  229.4 4.9 %custom-call.26 = f32[2,1,32,32]{2,3,1,0:T(8,128)S(1)} custom-call(f32[2,1,32,32]{3,2,1,0:T(8,128)S(1)} %select_bitcast_fusion.2), custom_call_target="InvertDiagBlocksLowerTriangular" | custom-call | tf_op jit(solution)/shard_map/while/body/eval_jaxpr/jit(_solve_triangular)/vmap()/triangular_solve | solution.py:40
  238.0 5.9 %custom-call.25 = f32[2,32,32]{2,1,0:T(8,128)S(1)} custom-call(f32[2,32,32]{2,1,0:T(8,128)S(1)} %fusion.337), custom_call_target="Cholesky" | custom-call | tf_op jit(solution)/shard_map/while/body/eval_jaxpr/jit(cholesky)/cholesky | solution.py:38
  244.1 4.9 %custom-call.26 = f32[2,1,32,32]{2,3,1,0:T(8,128)S(1)} custom-call(f32[2,1,32,32]{3,2,1,0:T(8,128)S(1)} %select_bitcast_fusion.2), custom_call_target="InvertDiagBlocksLowerTriangular" | custom-call | tf_op jit(solution)/shard_map/while/body/eval_jaxpr/jit(_solve_triangular)/vmap()/triangular_solve | solution.py:40
  253.3 0.6 copy-done.9
  255.3 17.1 %all_gather.23 = f32[16,2,64]{2,1,0:T(2,128)S(1)} all-gather(f32[1,2,64]{2,1,0:T(2,128)S(1)} %slice_add_fusion.8), channel_id=1, replica_groups=mesh['grp'=2,'tm'=16] {'tm'}, dimensions={0}, use_global_device_ids=true | all-gather | bytes 8704 | tf_op jit(solution)/shard_map/all_gather | solution.py:13
  272.7 22.2 %all-gather.1 = f32[32,64,64]{2,1,0:T(8,128)S(1)} all-gather(f32[2,64,64]{2,1,0:T(8,128)S(1)} %fusion.129), channel_id=3, replica_groups=mesh['grp'=2,'tm'=16] {'tm'}, dimensions={0}, use_global_device_ids=true | all-gather | bytes 557056 | tf_op jit(solution)/shard_map/all_gather | solution.py:13
  294.9 0.7 copy-done.13
  295.8 4.9 %while.73 = (s32[]{:T(128)}, f32[2,64]{1,0:T(2,128)S(1)}, f32[8,2,64]{2,1,0:T(2,128)S(1)}, f32[8,2,32]{2,1,0:T(2,128)S(1)}, f32[8,2,64,64]{3,2,1,0:T(8,128)S(1)}...) while((s32[]{:T(128)}, f32[2,64]{1,0:T(2,128)S(1)}, ...), condition=%wide.region_11.12_spmd, body=%wide.region_10.11_spmd.sunk | while | flops 196994 | bytes 143489 | solution.py:148
  300.9 37.0 %psum.7 = f32[2]{0:T(128)S(1)} all-reduce(f32[2]{0:T(128)S(1)} %reduce_sum.39), channel_id=1, replica_groups=mesh['grp'=2,'tm'=16] {'tm'}, use_global_device_ids=true, to_apply=%region_13.14 | all-reduce | flops 2 | bytes 16 | tf_op jit(solution)/shard_map/psum | solution.py:133
  (585 shorter events, 65.1 us)
Async XLA Ops:
  0.6 1.0 copy-start
  1.6 0.8 copy-start.4
  2.6 1.1 copy-start.1
  2.7 1.1 copy-start.2
  6.8 0.7 copy-start.5
  7.5 0.7 copy-start.7
  7.5 0.7 copy-start.8
  253.3 0.6 copy-start.9
  254.0 0.7 slice-start
  254.6 0.7 copy-start.10
  294.9 0.7 copy-start.13
  300.8 37.6 %copy-start.3 = (f32[8,2,32,64]{3,2,1,0:T(8,128)}, f32[8,2,32,64]{3,2,1,0:T(8,128)S(1)}, u32[]{:S(2)}) copy-start(f32[8,2,32,64]{3,2,1,0:T(8,128)S(1)} %get-tuple-element.1153) | copy-start | bytes 393220
  300.8 37.6 %copy-start.6 = (f32[8,2,32]{2,1,0:T(2,128)}, f32[8,2,32]{2,1,0:T(2,128)S(1)}, u32[]{:S(2)}) copy-start(f32[8,2,32]{2,1,0:T(2,128)S(1)} %get-tuple-element.1155) | copy-start | bytes 6148
  300.8 37.6 %copy-start.11 = (f32[8,2,32]{2,1,0:T(2,128)}, f32[8,2,32]{2,1,0:T(2,128)S(1)}, u32[]{:S(2)}) copy-start(f32[8,2,32]{2,1,0:T(2,128)S(1)} %get-tuple-element.532) | copy-start | bytes 6148
  300.8 37.6 %copy-start.12 = (f32[8,2,64]{2,1,0:T(2,128)}, f32[8,2,64]{2,1,0:T(2,128)S(1)}, u32[]{:S(2)}) copy-start(f32[8,2,64]{2,1,0:T(2,128)S(1)} %get-tuple-element.531) | copy-start | bytes 12292
where the time goes:
time: 340 us; the launch traced here: 339 us
  blocking collectives  161 us (47%)
  other arithmetic  92.6 us (27%)
  matrix products  74.1 us (22%)
  local copies, waits for them, and re-layouts  7.09 us (2%)
    all_gather x6, blocking collectives, carried_in(): gathered = jax.tree.map(lambda a: lax.all_gather(a, axis), part)  124 us
    dot_general x237, matrix products, product(): return jnp.matmul(left, right, precision=lax.Precision.HIGHEST)  70.7 us
    another operation x32, other arithmetic, spd_solve(): factor = jnp.linalg.cholesky(matrix)  48.2 us
    another operation x24, other arithmetic, spd_solve(): return jax.scipy.linalg.solve_triangular(factor, inner, lower=True, trans=1)  39.9 us
    psum x1, blocking collectives, shards(): decrease = lax.psum(jnp.sum(changes, 0), 'tm') / knots  37 us

commit v1 on v0

v1 whole, which is shorter than its diff:
```python
import functools
import math

import jax
import jax.numpy as jnp
from jax import lax
from jax.experimental import pallas as pl
from jax.experimental.pallas import tpu as pltpu
from jax.sharding import PartitionSpec as P

F32 = jnp.float32
BF16 = jnp.bfloat16
PAD = 8
MESH = pl.DeviceIdType.MESH
NN = (((1,), (0,)), ((), ()))
NT = (((1,), (1,)), ((), ()))


def split(a):
    hi = a.astype(BF16)
    return hi, (a - hi.astype(F32)).astype(BF16)


def dot3(a, b, dims=NN):
    ah, al = split(a)
    bh, bl = split(b)
    one = functools.partial(lax.dot_general, dimension_numbers=dims, preferred_element_type=F32)
    return one(ah, bh) + (one(ah, bl) + one(al, bh))


def with_row(matrix, row):
    first = lax.broadcasted_iota(jnp.int32, (PAD, row.shape[1]), 0) == 0
    return jnp.concatenate([matrix, jnp.where(first, row, 0.0)], 0)


def add_tail(a, tail):
    return jnp.concatenate([a[:-PAD], a[-PAD:] + tail], 0)


def compose_value(low, high):
    w = low.shape[1] // 2
    t = add_tail(dot3(low[:, :w], high[:w]), high[w:])
    right = dot3(t[:, w:], low[:w, :w], NT) + low[:, w:]
    return jnp.concatenate([t[:, :w], right], 1)


def apply_value(elem, value):
    w = value.shape[1]
    t = add_tail(dot3(elem[:, :w], value[:w]), value[w:])
    return dot3(t, elem[:w, :w], NT) + elem[:, w:]


def compose_state(low, high):
    w = low.shape[1]
    return add_tail(dot3(low, high[:w]), high[w:])


def place(tm):
    me = lax.axis_index("tm")
    rounds = tm.bit_length() - 1
    bits = [lax.rem(me // (1 << k), 2) for k in range(rounds)]
    partners = [me + (1 << k) * (1 - 2 * bits[k]) for k in range(rounds)]
    return bits, partners


def greet(partners):
    barrier = pltpu.get_barrier_semaphore()
    for partner in partners:
        pl.semaphore_signal(barrier, inc=1, device_id={"tm": partner}, device_id_type=MESH)


def greeted(partners):
    pl.semaphore_wait(pltpu.get_barrier_semaphore(), len(partners))


def exchange(src, dst, sems, k, partner):
    copy = pltpu.make_async_remote_copy(
        src_ref=src,
        dst_ref=dst,
        send_sem=sems.at[0, k],
        recv_sem=sems.at[1, k],
        device_id={"tm": partner},
        device_id_type=MESH,
    )
    copy.start()
    copy.wait()


def value_kernel(
    tm, a_ref, b_ref, k_ref, d_ref, sg_ref, cg_ref, cf_ref, rf_ref,
    elem_ref, end_ref, seg_ref, send_ref, recv_ref, psend_ref, precv_ref, sems,
):
    local, trajs, w, nu = b_ref.shape
    knots = local * tm
    scale = 1.0 / math.sqrt(knots)
    bits, partners = place(tm)
    greet(partners)
    eye = lambda n: (
        lax.broadcasted_iota(jnp.int32, (n, n), 0) == lax.broadcasted_iota(jnp.int32, (n, n), 1)
    ).astype(F32)
    term_q = eye(w) + dot3(cf_ref[...], cf_ref[...], NT)
    run_q = term_q / knots
    run_r = eye(nu) + dot3(rf_ref[...], rf_ref[...], NT)
    for t in range(local):
        for j in range(trajs):
            gain = k_ref[t, j]
            gain_t = gain.T
            g_mat = a_ref[t, j].T + dot3(gain_t, b_ref[t, j], NT)
            left = with_row(dot3(gain_t, run_r), cg_ref[t, j : j + 1])
            right = dot3(left, gain) + with_row(run_q, sg_ref[t, j : j + 1] * scale)
            elem_ref[t, j] = jnp.concatenate(
                [with_row(g_mat, d_ref[t, j : j + 1] * scale), right], 1
            )
    prev, base, count, at = elem_ref, 0, local, 0
    while count > 1:
        for i in range(count // 2):
            for j in range(trajs):
                seg_ref[at + i, j] = compose_value(prev[base + 2 * i, j], prev[base + 2 * i + 1, j])
        prev, base, at, count = seg_ref, at, at + count // 2, count // 2
    greeted(partners)
    totals = [prev[base, j] for j in range(trajs)]
    ident = with_row(
        jnp.concatenate([eye(w), jnp.zeros((w, w), F32)], 1), jnp.zeros((1, 2 * w), F32)
    )
    suffix = [ident] * trajs
    start = with_row(term_q, jnp.zeros((1, w), F32))
    last = len(partners) - 1
    for k in range(last):
        for j in range(trajs):
            send_ref[k, j] = totals[j]
        exchange(send_ref.at[k], recv_ref.at[k], sems, k, partners[k])
        up = bits[k] == 0
        for j in range(trajs):
            other = recv_ref[k, j]
            low = jnp.where(up, totals[j], other)
            high = jnp.where(up, other, totals[j])
            suffix[j] = jnp.where(up, compose_value(suffix[j], other), suffix[j])
            totals[j] = compose_value(low, high)
    if last >= 0:
        psend_ref[...] = jnp.concatenate([apply_value(totals[j], start) for j in range(trajs)], 1)
        exchange(psend_ref, precv_ref, sems, last, partners[last])
        up = bits[last] == 0
        for j in range(trajs):
            came = jnp.where(up, precv_ref[:, j * w : (j + 1) * w], start)
            end_ref[j] = apply_value(suffix[j], came)
    else:
        for j in range(trajs):
            end_ref[j] = start


def gain_kernel(
    knots, a_ref, b_ref, d_ref, cg_ref, rf_ref, elem_ref, seg_ref, end_ref,
    gain_ref, xt_ref, map_ref, fold_ref, tot_ref, val_ref, aug_ref,
):
    local, trajs, w, nu = b_ref.shape
    scale = 1.0 / math.sqrt(knots)
    eye = (
        lax.broadcasted_iota(jnp.int32, (nu, nu), 0) == lax.broadcasted_iota(jnp.int32, (nu, nu), 1)
    ).astype(F32)
    run_r = eye + dot3(rf_ref[...], rf_ref[...], NT)
    starts, count, at = [], local // 2, 0
    while count >= 1:
        starts.append(at)
        at += count
        count //= 2
    for j in range(trajs):
        val_ref[local - 1, j] = end_ref[j]
    half = local // 2
    while half >= 1:
        level = half.bit_length() - 1
        for i in range(local // (2 * half)):
            for j in range(trajs):
                hi = 2 * i + 1
                elem = elem_ref[hi, j] if level == 0 else seg_ref[starts[level - 1] + hi, j]
                val_ref[hi * half - 1, j] = apply_value(elem, val_ref[(hi + 1) * half - 1, j])
        half //= 2
    lane = lax.broadcasted_iota(jnp.int32, (nu, w + nu + PAD), 1)
    for t in range(local):
        cg_t = cg_ref[t].T
        for j in range(trajs):
            b_t = b_ref[t, j].T
            value = val_ref[t, j]
            rows = with_row(jnp.concatenate([a_ref[t, j].T, b_t], 0), d_ref[t, j : j + 1] * scale)
            y = add_tail(dot3(rows, value[:w]), value[w:])
            aug = dot3(b_t, y, NT)
            aug = aug + jnp.concatenate(
                [jnp.zeros((nu, w), F32), run_r, jnp.zeros((nu, PAD), F32)], 1
            )
            aug = jnp.where(lane == w + nu, aug + cg_t[:, j : j + 1], aug)
            aug_ref[t * trajs + j] = aug
    pairs = local * trajs
    group = min(8, pairs)
    sub = lax.broadcasted_iota(jnp.int32, (1, 8, 1), 1)
    for g0 in range(0, pairs, group):
        parts = [aug_ref[g0 : g0 + group, 8 * q : 8 * q + 8] for q in range(nu // 8)]
        for s in range(nu):
            q0, r0 = divmod(s, 8)
            pivot = parts[q0][:, r0 : r0 + 1]
            row = pivot / pivot[:, :, w + s : w + s + 1]
            for q in range(nu // 8):
                new = parts[q] - parts[q][:, :, w + s : w + s + 1] * row
                parts[q] = jnp.where(sub == r0, row, new) if q == q0 else new
        for g in range(group):
            t, j = divmod(g0 + g, trajs)
            x = jnp.concatenate([part[g] for part in parts], 0)
            gain_ref[t, j] = -x[:, :w]
            x_t = x.T
            xt = -jnp.concatenate([x_t[:w], x_t[w + nu :]], 0)
            xt_ref[t, j] = xt
            map_ref[t, j] = (
                dot3(xt, b_ref[t, j], NT) + with_row(a_ref[t, j].T, d_ref[t, j : j + 1] * scale)
            )
    prev, base, count, at = map_ref, 0, local, 0
    while count > 1:
        for i in range(count // 2):
            for j in range(trajs):
                fold_ref[at + i, j] = compose_state(
                    prev[base + 2 * i, j], prev[base + 2 * i + 1, j]
                )
        prev, base, at, count = fold_ref, at, at + count // 2, count // 2
    for j in range(trajs):
        tot_ref[0 : w + PAD, j * w : (j + 1) * w] = prev[base, j]
        total = jnp.zeros((nu, 1), F32)
        for t in range(local):
            aug = aug_ref[t * trajs + j]
            feed = xt_ref[t, j][w : w + 1]
            hess_feed = jnp.sum(aug[:, w : w + nu] * feed, 1, keepdims=True)
            back = dot3(eye, xt_ref[t, j][w:], NT)[:, :1]
            total = total + back * (aug[:, w + nu : w + nu + 1] + 0.5 * hess_feed)
        tot_ref[w + PAD :, j * w : (j + 1) * w] = jnp.broadcast_to(
            jnp.sum(total, 0, keepdims=True), (8, w)
        )


def state_kernel(
    tm, init_ref, xt_ref, map_ref, fold_ref, tot_ref,
    state_ref, control_ref, feed_ref, dec_ref, send_ref, recv_ref, sems,
):
    local, trajs, high, nu = xt_ref.shape
    w = high - PAD
    bits, partners = place(tm)
    greet(partners)
    for t in range(local):
        for j in range(trajs):
            feed_ref[t, j : j + 1] = xt_ref[t, j, w : w + 1]
    row0 = lax.broadcasted_iota(jnp.int32, (PAD, w), 0) == 0
    totals = [tot_ref[:high, j * w : (j + 1) * w] for j in range(trajs)]
    dec = tot_ref[high:]
    prefix = [jnp.where(row0, init_ref[j : j + 1], 0.0) for j in range(trajs)]
    ident = with_row(
        (
            lax.broadcasted_iota(jnp.int32, (w, w), 0) == lax.broadcasted_iota(jnp.int32, (w, w), 1)
        ).astype(F32),
        jnp.zeros((1, w), F32),
    )
    before = [ident] * trajs
    greeted(partners)
    for k in range(len(partners)):
        src = tot_ref
        if k > 0:
            for j in range(trajs):
                send_ref[k, :high, j * w : (j + 1) * w] = totals[j]
            send_ref[k, high:] = dec
            src = send_ref.at[k]
        exchange(src, recv_ref.at[k], sems, k, partners[k])
        dec = dec + recv_ref[k, high:]
        up = bits[k] == 0
        for j in range(trajs):
            other = recv_ref[k, :high, j * w : (j + 1) * w]
            before[j] = jnp.where(up, before[j], compose_state(other, before[j]))
            if k + 1 < len(partners):
                low = jnp.where(up, totals[j], other)
                top = jnp.where(up, other, totals[j])
                totals[j] = compose_state(low, top)
    starts, count, at = [], local // 2, 0
    while count >= 1:
        starts.append(at)
        at += count
        count //= 2
    for j in range(trajs):
        x = {0: dot3(prefix[j], before[j][:w]) + before[j][w:]}
        half = local // 2
        while half >= 1:
            level = half.bit_length() - 1
            for i in range(local // (2 * half)):
                elem = map_ref[2 * i, j] if level == 0 else fold_ref[starts[level - 1] + 2 * i, j]
                at_t = 2 * i * half
                x[at_t + half] = dot3(x[at_t], elem[:w]) + elem[w:]
            half //= 2
        for t in range(local):
            xt = xt_ref[t, j]
            state_ref[t, j : j + 1] = x[t][:1]
            control_ref[t, j : j + 1] = (dot3(x[t], xt[:w]) + xt[w:])[:1]
        dec_ref[j : j + 1] = dec[:1, j * w : (j + 1) * w] / (local * tm)


def shards(tm, dyn_a, dyn_b, gains, defects, state_grad, control_grad, cost_factor, control_factor, init_state):
    local, trajs, w, nu = dyn_b.shape
    high = w + PAD
    knots = local * tm
    rounds = tm.bit_length() - 1
    shape = lambda *s: jax.ShapeDtypeStruct(s, F32)
    vm = pl.BlockSpec(memory_space=pltpu.VMEM)
    elem, end, seg = pl.pallas_call(
        functools.partial(value_kernel, tm),
        out_shape=(shape(local, trajs, high, 2 * w), shape(trajs, high, w), shape(max(local - 1, 1), trajs, high, 2 * w)),
        in_specs=[vm] * 8,
        out_specs=(vm,) * 3,
        scratch_shapes=[
            pltpu.VMEM((max(rounds, 1), trajs, high, 2 * w), F32),
            pltpu.VMEM((max(rounds, 1), trajs, high, 2 * w), F32),
            pltpu.VMEM((high, trajs * w), F32),
            pltpu.VMEM((high, trajs * w), F32),
            pltpu.SemaphoreType.DMA((2, max(rounds, 1))),
        ],
        compiler_params=pltpu.CompilerParams(collective_id=0, has_side_effects=True),
        name="value",
    )(dyn_a, dyn_b, gains, defects, state_grad, control_grad, cost_factor, control_factor)
    new_gains, xt, maps, fold, tot = pl.pallas_call(
        functools.partial(gain_kernel, knots),
        out_shape=(
            shape(local, trajs, nu, w),
            shape(local, trajs, high, nu),
            shape(local, trajs, high, w),
            shape(max(local - 1, 1), trajs, high, w),
            shape(high + 8, trajs * w),
        ),
        in_specs=[vm] * 8,
        out_specs=(vm,) * 5,
        scratch_shapes=[
            pltpu.VMEM((local, trajs, high, w), F32),
            pltpu.VMEM((local * trajs, nu, w + nu + PAD), F32),
        ],
        name="gain",
    )(dyn_a, dyn_b, defects, control_grad, control_factor, elem, seg, end)
    states, controls, feed, dec = pl.pallas_call(
        functools.partial(state_kernel, tm),
        out_shape=(
            shape(local, trajs, w),
            shape(local, trajs, nu),
            shape(local, trajs, nu),
            shape(trajs, w),
        ),
        in_specs=[vm] * 5,
        out_specs=(vm,) * 4,
        scratch_shapes=[
            pltpu.VMEM((max(rounds, 1), high + 8, trajs * w), F32),
            pltpu.VMEM((max(rounds, 1), high + 8, trajs * w), F32),
            pltpu.SemaphoreType.DMA((2, max(rounds, 1))),
        ],
        compiler_params=pltpu.CompilerParams(collective_id=1, has_side_effects=True),
        name="state",
    )(init_state, xt, maps, fold, tot)
    return new_gains, feed, states, controls, dec[:, 0]


def solution(mesh):
    in_specs = (
        P("tm", "grp", None, None),
        P("tm", "grp", None, None),
        P("tm", "grp", None, None),
        P("tm", "grp", None),
        P("tm", "grp", None),
        P("tm", "grp", None),
        P(),
        P(),
        P("grp", None),
    )
    out_specs = (
        P("tm", "grp", None, None),
        P("tm", "grp", None),
        P("tm", "grp", None),
        P("tm", "grp", None),
        P("grp"),
    )
    return jax.shard_map(
        functools.partial(shards, mesh.shape["tm"]),
        mesh=mesh, in_specs=in_specs, out_specs=out_specs, check_vma=False,
    )
```

time: 340 us -> 62 us (0.18)
  blocking collectives: 161 us -> 0 us
  other arithmetic: 92.6 us -> 0 us
  matrix products: 74.1 us -> 0 us
  Pallas kernels: 0 us -> 55.7 us
    all_gather x6 -> x0, blocking collectives: 124 us -> none  [carried_in(): gathered = jax.tree.map(lambda a: lax.all_gather(a, axis), part)]
    another operation x56 -> x0, other arithmetic: 88.1 us -> none  [the longest x32 48.2 us: spd_solve(): factor = jnp.linalg.cholesky(matrix)]
    dot_general x237 -> x0, matrix products: 70.7 us -> none  [product(): return jnp.matmul(left, right, precision=lax.Precision.HIGHEST)]
    pallas_call x0 -> x3, Pallas kernels: none -> 55.7 us  [the longest x1 26 us: shards(): pl.pallas_call(functools.partial(value_kernel, tm), out_shape=(shape(loca...]
    psum x1 -> x0, blocking collectives: 37 us -> none  [shards(): decrease = lax.psum(jnp.sum(changes, 0), 'tm') / knots]
    another operation x16 -> x0, matrix products: 3.46 us -> none  [the longest x8 2.16 us: spd_solve(): inner = jax.scipy.linalg.solve_triangular(factor, right_side, lower=True)]
where the time goes in v1:
time: 62 us; the launch traced here: 61.7 us
  Pallas kernels  55.7 us (90%)
  local copies, waits for them, and re-layouts  5.28 us (9%)
  between operations  0.66 us (1%)
    pallas_call x1, Pallas kernels, shards(): pl.pallas_call(functools.partial(value_kernel, tm), out_shape=(shape(loca...  26 us
    pallas_call x1, Pallas kernels, shards(): pl.pallas_call(functools.partial(state_kernel, tm), out_shape=(shape(loca...  15 us
    pallas_call x1, Pallas kernels, shards(): pl.pallas_call(functools.partial(gain_kernel, knots), out_shape=(shape(lo...  14.7 us
    unnamed x10, local copies, waits for them, and re-layouts  3.98 us
    slice x1, local copies, waits for them, and re-layouts, shards(): return (new_gains, feed, states, controls, dec[:, 0])  1.3 us

profile of v1, /device:TPU:0, one launch (start us, length us, event | category | flops | bytes accessed | tf_op | source)
XLA Modules:
  0.0 61.7 jit_solution(2108715380630543288)
XLA Ops:
  0.6 2.0 %copy.17.b_ref = f32[8,2,64,32]{3,2,1,0:T(8,128)} copy(f32[8,2,64,32]{2,3,1,0:T(8,128)} %param.10) | data formatting | bytes 262144 | tf_op args[1]
  2.6 26.0 %value.1 = (f32[8,2,72,128]{3,2,1,0:T(8,128)}, f32[2,72,64]{2,1,0:T(8,128)}, f32[7,2,72,128]{3,2,1,0:T(8,128)}) custom-call(f32[8,2,64,64]{3,2,1,0:T(8,128)} %a_ref.3, f32[8,2,64,32]{3,2,1,0:T(8,128)} %copy.17.b_ref, f32[8,2,32,64]{3,2,1,0:T(8,128)} %k_ref.1, f32[8,2,64]{2,1,0:T(2,128)} %d_ref.3, f32[8,2,64]{2,1,0:T(2,128)} %sg_ref.1, f32[8,2,32]{2,1,0:T(2,128)} %cg_ref.3, ...), custom_call_target="tpu_custom_call" | custom-call | tf_op jit(solution)/shard_map/value/pallas_call | solution.py:304
  28.7 14.7 %gain.1 = (f32[8,2,32,64]{3,2,1,0:T(8,128)}, f32[8,2,72,32]{3,2,1,0:T(8,128)}, f32[8,2,72,64]{3,2,1,0:T(8,128)}, f32[7,2,72,64]{3,2,1,0:T(8,128)}, f32[80,128]{1,0:T(8,128)}) custom-call(f32[8,2,64,64]{3,2,1,0:T(8,128)} %a_ref.3, f32[8,2,64,32]{3,2,1,0:T(8,128)} %copy.17.b_ref, f32[8,2,64]{2,1,0:T(2,128)} %d_ref.3, f32[8,2,32]{2,1,0:T(2,128)} %cg_ref.3, ...), custom_call_target="tpu_custom_call" | custom-call | tf_op jit(solution)/shard_map/gain/pallas_call | solution.py:319
  43.3 15.0 %state.1 = (f32[8,2,64]{2,1,0:T(2,128)}, f32[8,2,32]{2,1,0:T(2,128)}, f32[8,2,32]{2,1,0:T(2,128)}, f32[2,64]{1,0:T(2,128)}) custom-call(f32[2,64]{1,0:T(2,128)} %init_ref.1, f32[8,2,72,32]{3,2,1,0:T(8,128)} %get-tuple-element.21.xt_ref, f32[8,2,72,64]{3,2,1,0:T(8,128)} %get-tuple-element.22.map_ref, f32[7,2,72,64]{3,2,1,0:T(8,128)} %get-tuple-element.23.fold_ref, ...), custom_call_target="tpu_custom_call" | custom-call | tf_op jit(solution)/shard_map/state/pallas_call | solution.py:336
  58.3 0.0 copy-start.2
  58.4 1.3 %slice_reduce_fusion = f32[2]{0:T(128)} fusion(f32[2,64]{1,0:T(2,128)} %get-tuple-element.28), kind=kLoop, calls=%fused_computation | loop fusion | bytes 16 | tf_op jit(solution)/shard_map/slice | solution.py:354
  59.7 0.0 copy-done.2
  59.7 0.0 copy-start.1
  59.7 0.6 copy.21
  60.3 0.1 copy-done.1
  60.4 0.0 copy-start
  60.4 0.6 copy.22
  61.0 0.1 copy-done
  61.1 0.6 copy.23
Async XLA Ops:
  58.3 1.3 %copy-start.2 = (f32[8,2,32]{2,1,0:T(2,128)S(1)}, f32[8,2,32]{2,1,0:T(2,128)}, u32[]{:S(2)}) copy-start(f32[8,2,32]{2,1,0:T(2,128)} %get-tuple-element.35) | copy-start | bytes 6148
  59.7 0.7 %copy-start.1 = (f32[8,2,64]{2,1,0:T(2,128)S(1)}, f32[8,2,64]{2,1,0:T(2,128)}, u32[]{:S(2)}) copy-start(f32[8,2,64]{2,1,0:T(2,128)} %get-tuple-element.36) | copy-start | bytes 12292
  60.4 0.7 %copy-start = (f32[8,2,32]{2,1,0:T(2,128)S(1)}, f32[8,2,32]{2,1,0:T(2,128)}, u32[]{:S(2)}) copy-start(f32[8,2,32]{2,1,0:T(2,128)} %get-tuple-element.37) | copy-start | bytes 6148

commit v2 on v1

--- a/solution.py
+++ b/solution.py
@@ -24,8 +24,9 @@
 def dot3(a, b, dims=NN):
     ah, al = split(a)
     bh, bl = split(b)
-    one = functools.partial(lax.dot_general, dimension_numbers=dims, preferred_element_type=F32)
-    return one(ah, bh) + (one(ah, bl) + one(al, bh))
+    left = jnp.concatenate([ah, al, ah], 1)
+    right = jnp.concatenate([bh, bh, bl], dims[0][1][0])
+    return lax.dot_general(left, right, dimension_numbers=dims, preferred_element_type=F32)
 
 
 def with_row(matrix, row):
@@ -87,10 +88,10 @@
 
 
 def value_kernel(
-    tm, a_ref, b_ref, k_ref, d_ref, sg_ref, cg_ref, cf_ref, rf_ref,
+    tm, a_ref, bt_ref, k_ref, d_ref, sg_ref, cg_ref, cf_ref, rf_ref,
     elem_ref, end_ref, seg_ref, send_ref, recv_ref, psend_ref, precv_ref, sems,
 ):
-    local, trajs, w, nu = b_ref.shape
+    local, trajs, nu, w = bt_ref.shape
     knots = local * tm
     scale = 1.0 / math.sqrt(knots)
     bits, partners = place(tm)
@@ -105,7 +106,7 @@
         for j in range(trajs):
             gain = k_ref[t, j]
             gain_t = gain.T
-            g_mat = a_ref[t, j].T + dot3(gain_t, b_ref[t, j], NT)
+            g_mat = a_ref[t, j].T + dot3(gain_t, bt_ref[t, j])
             left = with_row(dot3(gain_t, run_r), cg_ref[t, j : j + 1])
             right = dot3(left, gain) + with_row(run_q, sg_ref[t, j : j + 1] * scale)
             elem_ref[t, j] = jnp.concatenate(
@@ -149,10 +150,10 @@
 
 
 def gain_kernel(
-    knots, a_ref, b_ref, d_ref, cg_ref, rf_ref, elem_ref, seg_ref, end_ref,
-    gain_ref, xt_ref, map_ref, fold_ref, tot_ref, val_ref, aug_ref,
+    knots, a_ref, bt_ref, d_ref, cg_ref, rf_ref, elem_ref, seg_ref, end_ref,
+    gain_ref, feed_ref, xt_ref, map_ref, fold_ref, tot_ref, val_ref, aug_ref, sol_ref,
 ):
-    local, trajs, w, nu = b_ref.shape
+    local, trajs, nu, w = bt_ref.shape
     scale = 1.0 / math.sqrt(knots)
     eye = (
         lax.broadcasted_iota(jnp.int32, (nu, nu), 0) == lax.broadcasted_iota(jnp.int32, (nu, nu), 1)
@@ -174,11 +175,12 @@
                 elem = elem_ref[hi, j] if level == 0 else seg_ref[starts[level - 1] + hi, j]
                 val_ref[hi * half - 1, j] = apply_value(elem, val_ref[(hi + 1) * half - 1, j])
         half //= 2
+    pairs = local * trajs
     lane = lax.broadcasted_iota(jnp.int32, (nu, w + nu + PAD), 1)
     for t in range(local):
         cg_t = cg_ref[t].T
         for j in range(trajs):
-            b_t = b_ref[t, j].T
+            b_t = bt_ref[t, j]
             value = val_ref[t, j]
             rows = with_row(jnp.concatenate([a_ref[t, j].T, b_t], 0), d_ref[t, j : j + 1] * scale)
             y = add_tail(dot3(rows, value[:w]), value[w:])
@@ -187,28 +189,28 @@
                 [jnp.zeros((nu, w), F32), run_r, jnp.zeros((nu, PAD), F32)], 1
             )
             aug = jnp.where(lane == w + nu, aug + cg_t[:, j : j + 1], aug)
-            aug_ref[t * trajs + j] = aug
-    pairs = local * trajs
-    group = min(8, pairs)
-    sub = lax.broadcasted_iota(jnp.int32, (1, 8, 1), 1)
-    for g0 in range(0, pairs, group):
-        parts = [aug_ref[g0 : g0 + group, 8 * q : 8 * q + 8] for q in range(nu // 8)]
-        for s in range(nu):
-            q0, r0 = divmod(s, 8)
-            pivot = parts[q0][:, r0 : r0 + 1]
-            row = pivot / pivot[:, :, w + s : w + s + 1]
-            for q in range(nu // 8):
-                new = parts[q] - parts[q][:, :, w + s : w + s + 1] * row
-                parts[q] = jnp.where(sub == r0, row, new) if q == q0 else new
-        for g in range(group):
-            t, j = divmod(g0 + g, trajs)
-            x = jnp.concatenate([part[g] for part in parts], 0)
+            aug_ref[pl.ds(t * trajs + j, nu, stride=pairs)] = jnp.concatenate(
+                [aug, jnp.zeros((nu, w - nu - PAD), F32)], 1
+            )
+    parts = [aug_ref[i * pairs : (i + 1) * pairs] for i in range(nu)]
+    for s in range(nu):
+        row = parts[s] * (1.0 / parts[s][:, w + s : w + s + 1])
+        order = [(s + 1 + i) % nu for i in range(nu - 1)]
+        for i in order:
+            parts[i] = parts[i] - parts[i][:, w + s : w + s + 1] * row
+        parts[s] = row
+    for i in range(nu):
+        sol_ref[i * pairs : (i + 1) * pairs] = parts[i]
+    for t in range(local):
+        for j in range(trajs):
+            x = sol_ref[pl.ds(t * trajs + j, nu, stride=pairs)]
             gain_ref[t, j] = -x[:, :w]
             x_t = x.T
-            xt = -jnp.concatenate([x_t[:w], x_t[w + nu :]], 0)
+            xt = -jnp.concatenate([x_t[:w], x_t[w + nu : w + nu + PAD]], 0)
             xt_ref[t, j] = xt
+            feed_ref[t, j : j + 1] = xt[w : w + 1]
             map_ref[t, j] = (
-                dot3(xt, b_ref[t, j], NT) + with_row(a_ref[t, j].T, d_ref[t, j : j + 1] * scale)
+                dot3(xt, bt_ref[t, j]) + with_row(a_ref[t, j].T, d_ref[t, j : j + 1] * scale)
             )
     prev, base, count, at = map_ref, 0, local, 0
     while count > 1:
@@ -222,7 +224,7 @@
         tot_ref[0 : w + PAD, j * w : (j + 1) * w] = prev[base, j]
         total = jnp.zeros((nu, 1), F32)
         for t in range(local):
-            aug = aug_ref[t * trajs + j]
+            aug = aug_ref[pl.ds(t * trajs + j, nu, stride=pairs)]
             feed = xt_ref[t, j][w : w + 1]
             hess_feed = jnp.sum(aug[:, w : w + nu] * feed, 1, keepdims=True)
             back = dot3(eye, xt_ref[t, j][w:], NT)[:, :1]
@@ -232,53 +234,62 @@
         )
 
 
-def state_kernel(
-    tm, init_ref, xt_ref, map_ref, fold_ref, tot_ref,
-    state_ref, control_ref, feed_ref, dec_ref, send_ref, recv_ref, sems,
-):
-    local, trajs, high, nu = xt_ref.shape
-    w = high - PAD
+def state_kernel(tm, init_ref, tot_ref, start_ref, send_ref, recv_ref, xsend_ref, xrecv_ref, sems):
+    trajs, w = init_ref.shape
+    high = w + PAD
     bits, partners = place(tm)
     greet(partners)
-    for t in range(local):
-        for j in range(trajs):
-            feed_ref[t, j : j + 1] = xt_ref[t, j, w : w + 1]
-    row0 = lax.broadcasted_iota(jnp.int32, (PAD, w), 0) == 0
-    totals = [tot_ref[:high, j * w : (j + 1) * w] for j in range(trajs)]
+    row0 = lax.broadcasted_iota(jnp.int32, (PAD, trajs * w), 0) == 0
+    eye = (
+        lax.broadcasted_iota(jnp.int32, (w, w), 0) == lax.broadcasted_iota(jnp.int32, (w, w), 1)
+    ).astype(F32)
+    lanes = [slice(j * w, (j + 1) * w) for j in range(trajs)]
+    totals = [tot_ref[:high, lanes[j]] for j in range(trajs)]
     dec = tot_ref[high:]
-    prefix = [jnp.where(row0, init_ref[j : j + 1], 0.0) for j in range(trajs)]
-    ident = with_row(
-        (
-            lax.broadcasted_iota(jnp.int32, (w, w), 0) == lax.broadcasted_iota(jnp.int32, (w, w), 1)
-        ).astype(F32),
-        jnp.zeros((1, w), F32),
-    )
-    before = [ident] * trajs
+    init = [jnp.broadcast_to(init_ref[j : j + 1], (PAD, w)) for j in range(trajs)]
+    before = [with_row(eye, jnp.zeros((1, w), F32))] * trajs
     greeted(partners)
-    for k in range(len(partners)):
+    last = len(partners) - 1
+    for k in range(last):
         src = tot_ref
         if k > 0:
             for j in range(trajs):
-                send_ref[k, :high, j * w : (j + 1) * w] = totals[j]
+                send_ref[k, :high, lanes[j]] = totals[j]
             send_ref[k, high:] = dec
             src = send_ref.at[k]
         exchange(src, recv_ref.at[k], sems, k, partners[k])
         dec = dec + recv_ref[k, high:]
         up = bits[k] == 0
         for j in range(trajs):
-            other = recv_ref[k, :high, j * w : (j + 1) * w]
+            other = recv_ref[k, :high, lanes[j]]
             before[j] = jnp.where(up, before[j], compose_state(other, before[j]))
-            if k + 1 < len(partners):
-                low = jnp.where(up, totals[j], other)
-                top = jnp.where(up, other, totals[j])
-                totals[j] = compose_state(low, top)
+            low = jnp.where(up, totals[j], other)
+            top = jnp.where(up, other, totals[j])
+            totals[j] = compose_state(low, top)
+    if last >= 0:
+        ends = [dot3(init[j], totals[j][:w]) + totals[j][w:] for j in range(trajs)]
+        xsend_ref[...] = jnp.where(row0, jnp.concatenate(ends, 1), dec)
+        exchange(xsend_ref, xrecv_ref, sems, last, partners[last])
+        came = xrecv_ref[...]
+        dec = dec + came[1:2]
+        for j in range(trajs):
+            init[j] = jnp.where(
+                bits[last] == 0, init[j], jnp.broadcast_to(came[:1, lanes[j]], (PAD, w))
+            )
+    firsts = [dot3(init[j], before[j][:w]) + before[j][w:] for j in range(trajs)]
+    start_ref[...] = jnp.where(row0, jnp.concatenate(firsts, 1), dec)
+
+
+def rollout_kernel(knots, start_ref, xt_ref, map_ref, fold_ref, state_ref, control_ref, dec_ref):
+    local, trajs, high, nu = xt_ref.shape
+    w = high - PAD
     starts, count, at = [], local // 2, 0
     while count >= 1:
         starts.append(at)
         at += count
         count //= 2
     for j in range(trajs):
-        x = {0: dot3(prefix[j], before[j][:w]) + before[j][w:]}
+        x = {0: start_ref[:, j * w : (j + 1) * w]}
         half = local // 2
         while half >= 1:
             level = half.bit_length() - 1
@@ -291,13 +302,14 @@
             xt = xt_ref[t, j]
             state_ref[t, j : j + 1] = x[t][:1]
             control_ref[t, j : j + 1] = (dot3(x[t], xt[:w]) + xt[w:])[:1]
-        dec_ref[j : j + 1] = dec[:1, j * w : (j + 1) * w] / (local * tm)
+        dec_ref[j] = start_ref[1, j * w] / knots
 
 
 def shards(tm, dyn_a, dyn_b, gains, defects, state_grad, control_grad, cost_factor, control_factor, init_state):
     local, trajs, w, nu = dyn_b.shape
     high = w + PAD
     knots = local * tm
+    dyn_bt = jnp.swapaxes(dyn_b, 2, 3)
     rounds = tm.bit_length() - 1
     shape = lambda *s: jax.ShapeDtypeStruct(s, F32)
     vm = pl.BlockSpec(memory_space=pltpu.VMEM)
@@ -315,43 +327,49 @@
         ],
         compiler_params=pltpu.CompilerParams(collective_id=0, has_side_effects=True),
         name="value",
-    )(dyn_a, dyn_b, gains, defects, state_grad, control_grad, cost_factor, control_factor)
-    new_gains, xt, maps, fold, tot = pl.pallas_call(
+    )(dyn_a, dyn_bt, gains, defects, state_grad, control_grad, cost_factor, control_factor)
+    new_gains, feed, xt, maps, fold, tot = pl.pallas_call(
         functools.partial(gain_kernel, knots),
         out_shape=(
             shape(local, trajs, nu, w),
+            shape(local, trajs, nu),
             shape(local, trajs, high, nu),
             shape(local, trajs, high, w),
             shape(max(local - 1, 1), trajs, high, w),
             shape(high + 8, trajs * w),
         ),
         in_specs=[vm] * 8,
-        out_specs=(vm,) * 5,
+        out_specs=(vm,) * 6,
         scratch_shapes=[
             pltpu.VMEM((local, trajs, high, w), F32),
-            pltpu.VMEM((local * trajs, nu, w + nu + PAD), F32),
+            pltpu.VMEM((nu * local * trajs, 2 * w), F32),
+            pltpu.VMEM((nu * local * trajs, 2 * w), F32),
         ],
         name="gain",
-    )(dyn_a, dyn_b, defects, control_grad, control_factor, elem, seg, end)
-    states, controls, feed, dec = pl.pallas_call(
+    )(dyn_a, dyn_bt, defects, control_grad, control_factor, elem, seg, end)
+    start = pl.pallas_call(
         functools.partial(state_kernel, tm),
-        out_shape=(
-            shape(local, trajs, w),
-            shape(local, trajs, nu),
-            shape(local, trajs, nu),
-            shape(trajs, w),
-        ),
-        in_specs=[vm] * 5,
-        out_specs=(vm,) * 4,
+        out_shape=shape(PAD, trajs * w),
+        in_specs=[vm] * 2,
+        out_specs=vm,
         scratch_shapes=[
             pltpu.VMEM((max(rounds, 1), high + 8, trajs * w), F32),
             pltpu.VMEM((max(rounds, 1), high + 8, trajs * w), F32),
+            pltpu.VMEM((PAD, trajs * w), F32),
+            pltpu.VMEM((PAD, trajs * w), F32),
             pltpu.SemaphoreType.DMA((2, max(rounds, 1))),
         ],
         compiler_params=pltpu.CompilerParams(collective_id=1, has_side_effects=True),
         name="state",
-    )(init_state, xt, maps, fold, tot)
-    return new_gains, feed, states, controls, dec[:, 0]
+    )(init_state, tot)
+    states, controls, dec = pl.pallas_call(
+        functools.partial(rollout_kernel, knots),
+        out_shape=(shape(local, trajs, w), shape(local, trajs, nu), shape(trajs)),
+        in_specs=[vm] * 4,
+        out_specs=(vm, vm, pl.BlockSpec(memory_space=pltpu.SMEM)),
+        name="rollout",
+    )(start, xt, maps, fold)
+    return new_gains, feed, states, controls, dec
 
 
 def solution(mesh):

time: 62 us -> 58.5 us (0.944)
  local copies, waits for them, and re-layouts: 5.28 us -> 0 us
  Pallas kernels: 55.7 us -> 57.6 us
    unnamed x10 -> x0, local copies, waits for them, and re-layouts: 3.98 us -> none
    pallas_call x1, Pallas kernels: 26 us -> 28.8 us  [shards(): pl.pallas_call(functools.partial(value_kernel, tm), out_shape=(shape(loca...]
    pallas_call x1, Pallas kernels: 14.7 us -> 12.6 us  [shards(): pl.pallas_call(functools.partial(gain_kernel, knots), out_shape=(shape(lo...]
    slice x1 -> x0, local copies, waits for them, and re-layouts: 1.3 us -> none  [shards(): return (new_gains, feed, states, controls, dec[:, 0])]
    pallas_call x1 -> x2, Pallas kernels: 15 us -> 16.2 us  [the longest x1 13 us: shards(): pl.pallas_call(functools.partial(state_kernel, tm), out_shape=shape(PAD,...]
where the time goes in v2:
time: 58.5 us; the launch traced here: 58.3 us
  Pallas kernels  57.6 us (98%)
  between operations  0.65 us (1%)
    pallas_call x1, Pallas kernels, shards(): pl.pallas_call(functools.partial(value_kernel, tm), out_shape=(shape(loca...  28.8 us
    pallas_call x1, Pallas kernels, shards(): pl.pallas_call(functools.partial(state_kernel, tm), out_shape=shape(PAD,...  13 us
    pallas_call x1, Pallas kernels, shards(): pl.pallas_call(functools.partial(gain_kernel, knots), out_shape=(shape(lo...  12.6 us
    pallas_call x1, Pallas kernels, shards(): pl.pallas_call(functools.partial(rollout_kernel, knots), out_shape=(shape...  3.2 us

profile of v2, /device:TPU:0, one launch (start us, length us, event | category | flops | bytes accessed | tf_op | source)
XLA Modules:
  0.0 58.3 jit_solution(1080357810132921749)
XLA Ops:
  0.6 28.8 %value.1 = (f32[8,2,72,128]{3,2,1,0:T(8,128)}, f32[2,72,64]{2,1,0:T(8,128)}, f32[7,2,72,128]{3,2,1,0:T(8,128)}) custom-call(f32[8,2,64,64]{3,2,1,0:T(8,128)} %a_ref.3, f32[8,2,32,64]{3,2,1,0:T(8,128)} %bitcast.1, f32[8,2,32,64]{3,2,1,0:T(8,128)} %k_ref.1, f32[8,2,64]{2,1,0:T(2,128)} %d_ref.3, f32[8,2,64]{2,1,0:T(2,128)} %sg_ref.1, f32[8,2,32]{2,1,0:T(2,128)} %cg_ref.3, ...), custom_call_target="tpu_custom_call" | custom-call | tf_op jit(solution)/shard_map/value/pallas_call | solution.py:316
  29.5 12.6 %gain.1 = (f32[8,2,32,64]{3,2,1,0:T(8,128)}, f32[8,2,32]{2,1,0:T(2,128)}, f32[8,2,72,32]{3,2,1,0:T(8,128)}, f32[8,2,72,64]{3,2,1,0:T(8,128)}, f32[7,2,72,64]{3,2,1,0:T(8,128)}, /*index=5*/f32[80,128]{1,0:T(8,128)}) custom-call(f32[8,2,64,64]{3,2,1,0:T(8,128)} %a_ref.3, f32[8,2,32,64]{3,2,1,0:T(8,128)} %bitcast.2, f32[8,2,64]{2,1,0:T(2,128)} %d_ref.3, ...), custom_call_target="tpu_custom_call" | custom-call | tf_op jit(solution)/shard_map/gain/pallas_call | solution.py:331
  42.0 13.0 %state.1.start_ref = f32[8,128]{1,0:T(8,128)} custom-call(f32[2,64]{1,0:T(2,128)} %init_ref.1, f32[80,128]{1,0:T(8,128)} %get-tuple-element.22.tot_ref), custom_call_target="tpu_custom_call" | custom-call | tf_op jit(solution)/shard_map/state/pallas_call | solution.py:350
  55.1 3.2 %rollout.1 = (f32[8,2,64]{2,1,0:T(2,128)}, f32[8,2,32]{2,1,0:T(2,128)}, f32[2]{0:T(128)}) custom-call(f32[8,128]{1,0:T(8,128)} %state.1.start_ref, f32[8,2,72,32]{3,2,1,0:T(8,128)} %get-tuple-element.23.xt_ref, f32[8,2,72,64]{3,2,1,0:T(8,128)} %get-tuple-element.24.map_ref, f32[7,2,72,64]{3,2,1,0:T(8,128)} %get-tuple-element.25.fold_ref), custom_call_target="tpu_custom_call" | custom-call | tf_op jit(solution)/shard_map/rollout/pallas_call | solution.py:365

commit v3 on v2

v3 whole, which is shorter than its diff:
```python
import functools
import math

import jax
import jax.numpy as jnp
from jax import lax
from jax.experimental import pallas as pl
from jax.experimental.pallas import tpu as pltpu
from jax.sharding import PartitionSpec as P

F32 = jnp.float32
BF16 = jnp.bfloat16
PAD = 8
MESH = pl.DeviceIdType.MESH
NN = (((1,), (0,)), ((), ()))
NT = (((1,), (1,)), ((), ()))


def split(a):
    hi = a.astype(BF16)
    return hi, (a - hi.astype(F32)).astype(BF16)


def dot3(a, b, dims=NN):
    ah, al = split(a)
    bh, bl = split(b)
    left = jnp.concatenate([ah, al, ah], 1)
    right = jnp.concatenate([bh, bh, bl], dims[0][1][0])
    return lax.dot_general(left, right, dimension_numbers=dims, preferred_element_type=F32)


def with_row(matrix, row):
    first = lax.broadcasted_iota(jnp.int32, (PAD, row.shape[1]), 0) == 0
    return jnp.concatenate([matrix, jnp.where(first, row, 0.0)], 0)


def add_tail(a, tail):
    return jnp.concatenate([a[:-PAD], a[-PAD:] + tail], 0)


def compose_value(low, high):
    w = low.shape[1] // 2
    t = add_tail(dot3(low[:, :w], high[:w]), high[w:])
    right = dot3(t[:, w:], low[:w, :w], NT) + low[:, w:]
    return jnp.concatenate([t[:, :w], right], 1)


def apply_value(elem, value):
    w = value.shape[1]
    t = add_tail(dot3(elem[:, :w], value[:w]), value[w:])
    return dot3(t, elem[:w, :w], NT) + elem[:, w:]


def compose_state(low, high):
    w = low.shape[1]
    return add_tail(dot3(low, high[:w]), high[w:])


def place(tm):
    me = lax.axis_index("tm")
    rounds = tm.bit_length() - 1
    bits = [lax.rem(me // (1 << k), 2) for k in range(rounds)]
    partners = [me + (1 << k) * (1 - 2 * bits[k]) for k in range(rounds)]
    return bits, partners


def greet(partners):
    barrier = pltpu.get_barrier_semaphore()
    for partner in partners:
        pl.semaphore_signal(barrier, inc=1, device_id={"tm": partner}, device_id_type=MESH)


def greeted(partners):
    pl.semaphore_wait(pltpu.get_barrier_semaphore(), len(partners))


def send(src, dst, sems, k, partner):
    copy = pltpu.make_async_remote_copy(
        src_ref=src,
        dst_ref=dst,
        send_sem=sems.at[0, k],
        recv_sem=sems.at[1, k],
        device_id={"tm": partner},
        device_id_type=MESH,
    )
    copy.start()
    return copy


def eye_of(n):
    return (
        lax.broadcasted_iota(jnp.int32, (n, n), 0) == lax.broadcasted_iota(jnp.int32, (n, n), 1)
    ).astype(F32)


def fold(leaves, scratch, trajs, compose):
    levels = [leaves]
    at = 0
    while len(levels[-1]) > 1:
        prev = levels[-1]
        level = []
        for i in range(len(prev) // 2):
            (r0, i0), (r1, i1) = prev[2 * i], prev[2 * i + 1]
            for j in range(trajs):
                scratch[at, j] = compose(r0[i0, j], r1[i1, j])
            level.append((scratch, at))
            at += 1
        levels.append(level)
    return levels


def main_kernel(
    tm, a_ref, bt_ref, k_ref, d_ref, sg_ref, cg_ref, cf_ref, rf_ref, init_ref,
    gain_ref, out_ref,
    elem_ref, seg_ref, suf_ref, send_ref, recv_ref, psend_ref, precv_ref,
    rows_ref, const_ref, aug_ref, sol_ref, xt_ref, map_ref, fold_ref, pre_ref,
    ssend_ref, srecv_ref, xsend_ref, xrecv_ref, sems,
):
    local, trajs, nu, w = bt_ref.shape
    high = w + PAD
    knots = local * tm
    pairs = local * trajs
    scale = 1.0 / math.sqrt(knots)
    bits, partners = place(tm)
    greet(partners)
    last = len(partners) - 1
    lanes = [slice(j * w, (j + 1) * w) for j in range(trajs)]
    term_q = eye_of(w) + dot3(cf_ref[...], cf_ref[...], NT)
    run_q = term_q / knots
    run_r = eye_of(nu) + dot3(rf_ref[...], rf_ref[...], NT)
    for t in range(local):
        for j in range(trajs):
            gain = k_ref[t, j]
            gain_t = gain.T
            base = with_row(a_ref[t, j].T, d_ref[t, j : j + 1] * scale)
            rows_ref[t, j, :w] = base[:w]
            rows_ref[t, j, w : w + nu] = bt_ref[t, j]
            rows_ref[t, j, w + nu :] = base[w:]
            g_mat = base[:w] + dot3(gain_t, bt_ref[t, j])
            left = with_row(dot3(gain_t, run_r), cg_ref[t, j : j + 1])
            right = dot3(left, gain) + with_row(run_q, sg_ref[t, j : j + 1] * scale)
            elem_ref[t, j] = jnp.concatenate(
                [jnp.concatenate([g_mat, base[w:]], 0), right], 1
            )
    levels = fold([(elem_ref, t) for t in range(local)], seg_ref, trajs, compose_value)

    def suffixes():
        for t in reversed(range(local - 1)):
            level = ((t + 1) & -(t + 1)).bit_length() - 1
            ref, i = levels[level][(t + 1) >> level]
            end = t + 1 + (1 << level)
            for j in range(trajs):
                whole = ref[i, j]
                suf_ref[t, j] = whole if end == local else compose_value(whole, suf_ref[end - 1, j])

    lane = lax.broadcasted_iota(jnp.int32, (nu, w + nu + PAD), 1)

    def constants(lo, hi):
        for t in range(lo, hi):
            cg_t = cg_ref[t].T
            for j in range(trajs):
                own = jnp.concatenate(
                    [jnp.zeros((nu, w), F32), run_r, jnp.zeros((nu, PAD), F32)], 1
                )
                own = jnp.where(lane == w + nu, own + cg_t[:, j : j + 1], own)
                if t < local - 1:
                    suf = suf_ref[t, j]
                    z = add_tail(dot3(rows_ref[t, j], suf[:w]), suf[w:])
                    rows_ref[t, j] = z[:, :w]
                    own = own + dot3(bt_ref[t, j], z[:, w:], NT)
                const_ref[t, j] = own

    def value_work(k):
        if k == max(last - 2, 0):
            suffixes()
        if k == max(last - 1, 0):
            constants(0, local // 2)
        if k == last:
            constants(local // 2, local)

    greeted(partners)
    ref, i = levels[-1][0]
    totals = [ref[i, j] for j in range(trajs)]
    ident = with_row(
        jnp.concatenate([eye_of(w), jnp.zeros((w, w), F32)], 1), jnp.zeros((1, 2 * w), F32)
    )
    suffix = [ident] * trajs
    start = with_row(term_q, jnp.zeros((1, w), F32))
    for k in range(last):
        for j in range(trajs):
            send_ref[k, j] = totals[j]
        copy = send(send_ref.at[k], recv_ref.at[k], sems, k, partners[k])
        value_work(k)
        copy.wait()
        up = bits[k] == 0
        for j in range(trajs):
            other = recv_ref[k, j]
            suffix[j] = jnp.where(up, compose_value(suffix[j], other), suffix[j])
            totals[j] = compose_value(
                jnp.where(up, totals[j], other), jnp.where(up, other, totals[j])
            )
    psend_ref[...] = jnp.concatenate([apply_value(totals[j], start) for j in range(trajs)], 1)
    copy = send(psend_ref, precv_ref, sems, last, partners[last])
    value_work(last)
    copy.wait()
    up = bits[last] == 0
    ends = [
        apply_value(suffix[j], jnp.where(up, precv_ref[:, lanes[j]], start)) for j in range(trajs)
    ]
    for t in range(local):
        for j in range(trajs):
            rows = rows_ref[t, j]
            y = add_tail(dot3(rows, ends[j][:w]), ends[j][w:])
            aug = dot3(rows[w : w + nu], y, NT) + const_ref[t, j]
            aug_ref[pl.ds(t * trajs + j, nu, stride=pairs)] = jnp.concatenate(
                [aug, jnp.zeros((nu, w - nu - PAD), F32)], 1
            )
    parts = [aug_ref[i * pairs : (i + 1) * pairs] for i in range(nu)]
    for s in range(nu):
        row = parts[s] * (1.0 / parts[s][:, w + s : w + s + 1])
        for i in [(s + 1 + i) % nu for i in range(nu - 1)]:
            parts[i] = parts[i] - parts[i][:, w + s : w + s + 1] * row
        parts[s] = row
    for i in range(nu):
        sol_ref[i * pairs : (i + 1) * pairs] = parts[i]
    for t in range(local):
        for j in range(trajs):
            x = sol_ref[pl.ds(t * trajs + j, nu, stride=pairs)]
            gain_ref[t, j] = -x[:, :w]
            x_t = x.T
            xt = -jnp.concatenate([x_t[:w], x_t[w + nu : w + nu + PAD]], 0)
            xt_ref[t, j] = xt
            map_ref[t, j] = (
                dot3(xt, bt_ref[t, j]) + with_row(a_ref[t, j].T, d_ref[t, j : j + 1] * scale)
            )
    maps = fold([(map_ref, t) for t in range(local)], fold_ref, trajs, compose_state)
    ref, i = maps[-1][0]
    totals = [ref[i, j] for j in range(trajs)]
    decs = []
    for j in range(trajs):
        total = jnp.zeros((nu, 1), F32)
        for t in range(local):
            aug = aug_ref[pl.ds(t * trajs + j, nu, stride=pairs)]
            sol = sol_ref[pl.ds(t * trajs + j, nu, stride=pairs)]
            feed = xt_ref[t, j, w : w + 1]
            hess_feed = jnp.sum(aug[:, w : w + nu] * feed, 1, keepdims=True)
            total = total - sol[:, w + nu : w + nu + 1] * (
                aug[:, w + nu : w + nu + 1] + 0.5 * hess_feed
            )
        decs.append(jnp.broadcast_to(jnp.sum(total, 0, keepdims=True), (PAD, w)))
    dec = jnp.concatenate(decs, 1)

    def prefixes():
        for t in range(local):
            for j in range(trajs):
                xt = xt_ref[t, j]
                if t == 0:
                    pre = with_row(eye_of(w), jnp.zeros((1, w), F32))
                    control = xt
                else:
                    level = (t & -t).bit_length() - 1
                    first = t - (1 << level)
                    ref, i = maps[level][first >> level]
                    pre = ref[i, j]
                    if first > 0:
                        pre = compose_state(pre_ref[first, j, :, :w], pre)
                    control = add_tail(dot3(pre, xt[:w]), xt[w:])
                pre_ref[t, j, :, :w] = pre
                pre_ref[t, j, :, w : w + nu] = control

    row0 = lax.broadcasted_iota(jnp.int32, (PAD, trajs * w), 0) == 0
    init = [jnp.broadcast_to(init_ref[j : j + 1], (PAD, w)) for j in range(trajs)]
    before = [with_row(eye_of(w), jnp.zeros((1, w), F32))] * trajs
    off = last + 1
    for k in range(last):
        for j in range(trajs):
            ssend_ref[k, :high, lanes[j]] = totals[j]
        ssend_ref[k, high:] = dec
        copy = send(ssend_ref.at[k], srecv_ref.at[k], sems, off + k, partners[k])
        if k == max(last - 1, 0):
            prefixes()
        copy.wait()
        dec = dec + srecv_ref[k, high:]
        up = bits[k] == 0
        for j in range(trajs):
            other = srecv_ref[k, :high, lanes[j]]
            before[j] = jnp.where(up, before[j], compose_state(other, before[j]))
            totals[j] = compose_state(
                jnp.where(up, totals[j], other), jnp.where(up, other, totals[j])
            )
    if last == 0:
        prefixes()
    tails = [dot3(init[j], totals[j][:w]) + totals[j][w:] for j in range(trajs)]
    xsend_ref[...] = jnp.where(row0, jnp.concatenate(tails, 1), dec)
    send(xsend_ref, xrecv_ref, sems, off + last, partners[last]).wait()
    came = xrecv_ref[...]
    dec = dec + came[1:2]
    out_ref[pairs:] = dec / knots
    for j in range(trajs):
        first = jnp.where(
            bits[last] == 0, init[j], jnp.broadcast_to(came[:1, lanes[j]], (PAD, w))
        )
        first = dot3(first, before[j][:w]) + before[j][w : w + 1]
        for t in range(local):
            pre = pre_ref[t, j, :, : w + nu]
            both = dot3(first, pre[:w]) + pre[w : w + 1]
            p = t * trajs + j
            out_ref[p : p + 1, : w + nu] = both[:1]
            out_ref[p : p + 1, w + nu : w + 2 * nu] = xt_ref[t, j, w : w + 1]


def unpack_kernel(gain_in, out_in, gain_ref, feed_ref, state_ref, control_ref, dec_ref):
    local, trajs, nu, w = gain_in.shape
    gain_ref[...] = gain_in[...]
    for t in range(local):
        at = slice(t * trajs, (t + 1) * trajs)
        state_ref[t] = out_in[at, :w]
        control_ref[t] = out_in[at, w : w + nu]
        feed_ref[t] = out_in[at, w + nu : w + 2 * nu]
    for j in range(trajs):
        dec_ref[j] = out_in[local * trajs, j * w]


def shards(tm, dyn_a, dyn_b, gains, defects, state_grad, control_grad, cost_factor, control_factor, init_state):
    local, trajs, w, nu = dyn_b.shape
    high = w + PAD
    pairs = local * trajs
    rounds = tm.bit_length() - 1
    shape = lambda *s: jax.ShapeDtypeStruct(s, F32)
    vmem = lambda *s: pltpu.VMEM(s, F32)
    vm = pl.BlockSpec(memory_space=pltpu.VMEM)
    new_gains, out = pl.pallas_call(
        functools.partial(main_kernel, tm),
        out_shape=(shape(local, trajs, nu, w), shape(pairs + PAD, trajs * w)),
        in_specs=[vm] * 9,
        out_specs=(vm, vm),
        scratch_shapes=[
            vmem(local, trajs, high, 2 * w),
            vmem(local, trajs, high, 2 * w),
            vmem(local, trajs, high, 2 * w),
            vmem(rounds, trajs, high, 2 * w),
            vmem(rounds, trajs, high, 2 * w),
            vmem(high, trajs * w),
            vmem(high, trajs * w),
            vmem(local, trajs, w + nu + PAD, w),
            vmem(local, trajs, nu, w + nu + PAD),
            vmem(nu * pairs, 2 * w),
            vmem(nu * pairs, 2 * w),
            vmem(local, trajs, high, nu),
            vmem(local, trajs, high, w),
            vmem(local, trajs, high, w),
            vmem(local, trajs, high, 2 * w),
            vmem(rounds, high + PAD, trajs * w),
            vmem(rounds, high + PAD, trajs * w),
            vmem(PAD, trajs * w),
            vmem(PAD, trajs * w),
            pltpu.SemaphoreType.DMA((2, 2 * rounds)),
        ],
        compiler_params=pltpu.CompilerParams(collective_id=0, has_side_effects=True),
        name="main",
    )(
        dyn_a, jnp.swapaxes(dyn_b, 2, 3), gains, defects, state_grad, control_grad,
        cost_factor, control_factor, init_state,
    )
    new_gains, feed, states, controls, dec = pl.pallas_call(
        unpack_kernel,
        out_shape=(
            shape(local, trajs, nu, w),
            shape(local, trajs, nu),
            shape(local, trajs, w),
            shape(local, trajs, nu),
            shape(trajs),
        ),
        in_specs=[vm] * 2,
        out_specs=(vm,) * 4 + (pl.BlockSpec(memory_space=pltpu.SMEM),),
        name="unpack",
    )(new_gains, out)
    return new_gains, feed, states, controls, dec


def solution(mesh):
    in_specs = (
        P("tm", "grp", None, None),
        P("tm", "grp", None, None),
        P("tm", "grp", None, None),
        P("tm", "grp", None),
        P("tm", "grp", None),
        P("tm", "grp", None),
        P(),
        P(),
        P("grp", None),
    )
    out_specs = (
        P("tm", "grp", None, None),
        P("tm", "grp", None),
        P("tm", "grp", None),
        P("tm", "grp", None),
        P("grp"),
    )
    return jax.shard_map(
        functools.partial(shards, mesh.shape["tm"]),
        mesh=mesh, in_specs=in_specs, out_specs=out_specs, check_vma=False,
    )
```

time: 58.5 us -> 48.2 us (0.82)
  Pallas kernels: 57.6 us -> 47.4 us
    pallas_call x4 -> x2, Pallas kernels: 57.6 us -> 47.4 us  [the longest x1 45.7 us: shards(): pl.pallas_call(functools.partial(main_kernel, tm), out_shape=(shape(local...]
where the time goes in v3:
time: 48.2 us; the launch traced here: 48.1 us
  Pallas kernels  47.4 us (98%)
  between operations  0.64 us (1%)
    pallas_call x1, Pallas kernels, shards(): pl.pallas_call(functools.partial(main_kernel, tm), out_shape=(shape(local...  45.7 us
    pallas_call x1, Pallas kernels, shards(): pl.pallas_call(unpack_kernel, out_shape=(shape(local, trajs, nu, w), shap...  1.69 us

profile of v3, /device:TPU:0, one launch (start us, length us, event | category | flops | bytes accessed | tf_op | source)
XLA Modules:
  0.0 48.1 jit_solution(7718942990637455778)
XLA Ops:
  0.6 45.7 %main.1 = (f32[8,2,32,64]{3,2,1,0:T(8,128)}, f32[24,128]{1,0:T(8,128)}) custom-call(f32[8,2,64,64]{3,2,1,0:T(8,128)} %a_ref.1, f32[8,2,32,64]{3,2,1,0:T(8,128)} %bitcast.1, f32[8,2,32,64]{3,2,1,0:T(8,128)} %k_ref.1, f32[8,2,64]{2,1,0:T(2,128)} %d_ref.1, f32[8,2,64]{2,1,0:T(2,128)} %sg_ref.1, f32[8,2,32]{2,1,0:T(2,128)} %cg_ref.1, f32[64,64]{1,0:T(8,128)} %cf_ref.1, ...), custom_call_target="tpu_custom_call" | custom-call | tf_op jit(solution)/shard_map/main/pallas_call | solution.py:332
  46.4 1.7 %unpack.1 = (f32[8,2,32,64]{3,2,1,0:T(8,128)}, f32[8,2,32]{2,1,0:T(2,128)}, f32[8,2,64]{2,1,0:T(2,128)}, f32[8,2,32]{2,1,0:T(2,128)}, f32[2]{0:T(128)}) custom-call(f32[8,2,32,64]{3,2,1,0:T(8,128)} %get-tuple-element.7.gain_in, f32[24,128]{1,0:T(8,128)} %get-tuple-element.8.out_in), custom_call_target="tpu_custom_call" | custom-call | tf_op jit(solution)/shard_map/unpack/pallas_call | solution.py:365

commit v4 on v3

--- a/solution.py
+++ b/solution.py
@@ -21,12 +21,22 @@
     return hi, (a - hi.astype(F32)).astype(BF16)
 
 
+def stack_left(a):
+    hi, lo = split(a)
+    return jnp.concatenate([hi, lo, hi], 1)
+
+
+def stack_right(b, axis=0):
+    hi, lo = split(b)
+    return jnp.concatenate([hi, hi, lo], axis)
+
+
+def mul3(left, right, dims=NN):
+    return lax.dot_general(left, right, dimension_numbers=dims, preferred_element_type=F32)
+
+
 def dot3(a, b, dims=NN):
-    ah, al = split(a)
-    bh, bl = split(b)
-    left = jnp.concatenate([ah, al, ah], 1)
-    right = jnp.concatenate([bh, bh, bl], dims[0][1][0])
-    return lax.dot_general(left, right, dimension_numbers=dims, preferred_element_type=F32)
+    return mul3(stack_left(a), stack_right(b, dims[0][1][0]), dims)
 
 
 def with_row(matrix, row):
@@ -114,7 +124,7 @@
     gain_ref, out_ref,
     elem_ref, seg_ref, suf_ref, send_ref, recv_ref, psend_ref, precv_ref,
     rows_ref, const_ref, aug_ref, sol_ref, xt_ref, map_ref, fold_ref, pre_ref,
-    ssend_ref, srecv_ref, xsend_ref, xrecv_ref, sems,
+    ssend_ref, srecv_ref, xsend_ref, xrecv_ref, base_ref, rows3_ref, pre3_ref, sems,
 ):
     local, trajs, nu, w = bt_ref.shape
     high = w + PAD
@@ -133,6 +143,7 @@
             gain = k_ref[t, j]
             gain_t = gain.T
             base = with_row(a_ref[t, j].T, d_ref[t, j : j + 1] * scale)
+            base_ref[t, j] = base
             rows_ref[t, j, :w] = base[:w]
             rows_ref[t, j, w : w + nu] = bt_ref[t, j]
             rows_ref[t, j, w + nu :] = base[w:]
@@ -166,8 +177,10 @@
                 if t < local - 1:
                     suf = suf_ref[t, j]
                     z = add_tail(dot3(rows_ref[t, j], suf[:w]), suf[w:])
-                    rows_ref[t, j] = z[:, :w]
+                    rows3_ref[t, j] = stack_left(z[:, :w])
                     own = own + dot3(bt_ref[t, j], z[:, w:], NT)
+                else:
+                    rows3_ref[t, j] = stack_left(rows_ref[t, j])
                 const_ref[t, j] = own
 
     def value_work(k):
@@ -207,11 +220,12 @@
     ends = [
         apply_value(suffix[j], jnp.where(up, precv_ref[:, lanes[j]], start)) for j in range(trajs)
     ]
+    rights = [stack_right(end[:w]) for end in ends]
     for t in range(local):
         for j in range(trajs):
-            rows = rows_ref[t, j]
-            y = add_tail(dot3(rows, ends[j][:w]), ends[j][w:])
-            aug = dot3(rows[w : w + nu], y, NT) + const_ref[t, j]
+            rows = rows3_ref[t, j]
+            y = add_tail(mul3(rows, rights[j]), ends[j][w:])
+            aug = mul3(rows[w : w + nu], stack_right(y, 1), NT) + const_ref[t, j]
             aug_ref[pl.ds(t * trajs + j, nu, stride=pairs)] = jnp.concatenate(
                 [aug, jnp.zeros((nu, w - nu - PAD), F32)], 1
             )
@@ -231,7 +245,7 @@
             xt = -jnp.concatenate([x_t[:w], x_t[w + nu : w + nu + PAD]], 0)
             xt_ref[t, j] = xt
             map_ref[t, j] = (
-                dot3(xt, bt_ref[t, j]) + with_row(a_ref[t, j].T, d_ref[t, j : j + 1] * scale)
+                dot3(xt, bt_ref[t, j]) + base_ref[t, j]
             )
     maps = fold([(map_ref, t) for t in range(local)], fold_ref, trajs, compose_state)
     ref, i = maps[-1][0]
@@ -267,6 +281,7 @@
                     control = add_tail(dot3(pre, xt[:w]), xt[w:])
                 pre_ref[t, j, :, :w] = pre
                 pre_ref[t, j, :, w : w + nu] = control
+                pre3_ref[t, j] = stack_right(jnp.concatenate([pre[:w], control[:w]], 1))
 
     row0 = lax.broadcasted_iota(jnp.int32, (PAD, trajs * w), 0) == 0
     init = [jnp.broadcast_to(init_ref[j : j + 1], (PAD, w)) for j in range(trajs)]
@@ -300,10 +315,9 @@
         first = jnp.where(
             bits[last] == 0, init[j], jnp.broadcast_to(came[:1, lanes[j]], (PAD, w))
         )
-        first = dot3(first, before[j][:w]) + before[j][w : w + 1]
+        left = stack_left(dot3(first, before[j][:w]) + before[j][w : w + 1])
         for t in range(local):
-            pre = pre_ref[t, j, :, : w + nu]
-            both = dot3(first, pre[:w]) + pre[w : w + 1]
+            both = mul3(left, pre3_ref[t, j]) + pre_ref[t, j, w : w + 1, : w + nu]
             p = t * trajs + j
             out_ref[p : p + 1, : w + nu] = both[:1]
             out_ref[p : p + 1, w + nu : w + 2 * nu] = xt_ref[t, j, w : w + 1]
@@ -354,6 +368,9 @@
             vmem(rounds, high + PAD, trajs * w),
             vmem(PAD, trajs * w),
             vmem(PAD, trajs * w),
+            vmem(local, trajs, high, w),
+            pltpu.VMEM((local, trajs, w + nu + PAD, 3 * w), BF16),
+            pltpu.VMEM((local, trajs, 3 * w, w + nu), BF16),
             pltpu.SemaphoreType.DMA((2, 2 * rounds)),
         ],
         compiler_params=pltpu.CompilerParams(collective_id=0, has_side_effects=True),

time: 48.2 us -> 48.4 us (level)
  no operation moved by 1% of the time
where the time goes in v4:
time: 48.4 us; the launch traced here: 48.3 us
  Pallas kernels  47.6 us (98%)
  between operations  0.64 us (1%)
    pallas_call x1, Pallas kernels, shards(): pl.pallas_call(functools.partial(main_kernel, tm), out_shape=(shape(local...  45.9 us
    pallas_call x1, Pallas kernels, shards(): pl.pallas_call(unpack_kernel, out_shape=(shape(local, trajs, nu, w), shap...  1.69 us

profile of v4, /device:TPU:0, one launch (start us, length us, event | category | flops | bytes accessed | tf_op | source)
XLA Modules:
  0.0 48.3 jit_solution(5589166310060678419)
XLA Ops:
  0.6 45.9 %main.1 = (f32[8,2,32,64]{3,2,1,0:T(8,128)}, f32[24,128]{1,0:T(8,128)}) custom-call(f32[8,2,64,64]{3,2,1,0:T(8,128)} %a_ref.1, f32[8,2,32,64]{3,2,1,0:T(8,128)} %bitcast.1, f32[8,2,32,64]{3,2,1,0:T(8,128)} %k_ref.1, f32[8,2,64]{2,1,0:T(2,128)} %d_ref.1, f32[8,2,64]{2,1,0:T(2,128)} %sg_ref.1, f32[8,2,32]{2,1,0:T(2,128)} %cg_ref.1, f32[64,64]{1,0:T(8,128)} %cf_ref.1, ...), custom_call_target="tpu_custom_call" | custom-call | tf_op jit(solution)/shard_map/main/pallas_call | solution.py:346
  46.6 1.7 %unpack.1 = (f32[8,2,32,64]{3,2,1,0:T(8,128)}, f32[8,2,32]{2,1,0:T(2,128)}, f32[8,2,64]{2,1,0:T(2,128)}, f32[8,2,32]{2,1,0:T(2,128)}, f32[2]{0:T(128)}) custom-call(f32[8,2,32,64]{3,2,1,0:T(8,128)} %get-tuple-element.7.gain_in, f32[24,128]{1,0:T(8,128)} %get-tuple-element.8.out_in), custom_call_target="tpu_custom_call" | custom-call | tf_op jit(solution)/shard_map/unpack/pallas_call | solution.py:382
